TPU v7x, 128 devices: a whole 4x4x4 slice. The times are simulated.
128 devices in a mesh: layer: 4 (over z_lo, core), row: 8 (over z_hi, y), col: 4 (over x).
Axes of the slice: x: 4, y: 4, z: 4 (z_hi: 2, z_lo: 2; z = z_hi * 2 + z_lo), core: 2. Of those that a mesh axis runs over, the one named last changes fastest.
Arguments:
- grad: bfloat16 [32768, 8192], P(('layer', 'row'), 'col'), parts along dimension 0, may hold values from -6 to 6
- error: bfloat16 [32768, 8192], P(('layer', 'row'), 'col'), parts along dimension 0, may hold values from -2 to 2
- left_old: bfloat16 [32768, 512], P(('layer', 'row')), parts along dimension 0, may hold values from -0.25 to 0.25
- right_old: bfloat16 [32768, 512], P(('layer', 'col')), parts along dimension 0, may hold values from -0.25 to 0.25
- first_old: float32 [2048, 512], P('layer'), parts along dimension 0, may hold values from -3 to 3
- second_old: float32 [2048, 512], P('layer'), parts along dimension 0, may hold values from 0.05 to 1
Outputs:
- error_new: bfloat16 [32768, 8192], P(('layer', 'row'), 'col'), parts along dimension 0
- first_moment: float32 [2048, 512], P('layer'), parts along dimension 0
- second_moment: float32 [2048, 512], P('layer'), parts along dimension 0
- update: float32 [2048, 512], P('layer'), parts along dimension 0
There are 4 independent parts, one for each index of `layer`. A program takes and returns all parts, laid end to end along the dimension named above; each array names one. Nothing has to cross between parts.
All inputs are finite; a program needn't handle non-finite values.
Results may differ from a plain program's by a relative error of at most 0.0075.
Values may be sent and summed in bfloat16 or wider, within the bound.
No kernel may reach another device: no remote copies, remote signals or barrier semaphores. Data moves between devices by JAX's collectives and lax.ppermute only.
A program may use at most 128 MiB of HBM per device.

v0:
```python
import jax
import jax.numpy as jnp
from jax import lax
from jax.sharding import PartitionSpec as P


def solve_rows(image, gram):
    factor = jnp.linalg.cholesky(gram)
    return jax.scipy.linalg.solve_triangular(factor, image.T, lower=True).T.astype(jnp.bfloat16)


def gram_of(image):
    return lax.dot_general(image, image, (((0,), (0,)), ((), ())), precision=lax.Precision.HIGH)


def split_pair(values):
    upper = values.astype(jnp.bfloat16)
    lower = (values - upper.astype(jnp.float32)).astype(jnp.bfloat16)
    return (upper, lower)


def per_device(grad, error, left_old, right_old, first_old, second_old):
    highest = lax.Precision.HIGHEST
    across = (((0,), (0,)), ((), ()))
    left_image = lax.psum(jnp.dot(grad, right_old, preferred_element_type=jnp.float32), "col")
    left_gram = lax.psum(gram_of(left_image), "row")
    left_basis = solve_rows(left_image, left_gram)
    right_part = lax.dot_general(grad, left_basis, across, preferred_element_type=jnp.float32)
    right_image = lax.psum(right_part, "row")
    right_gram = lax.psum(gram_of(right_image), "col")
    right_basis = solve_rows(right_image, right_gram)
    summed = grad.astype(jnp.float32) + error.astype(jnp.float32)
    accum = summed.astype(jnp.bfloat16)
    carried = jnp.dot(accum, right_basis, preferred_element_type=jnp.float32)
    carried_upper, carried_lower = split_pair(carried)
    core_part = lax.dot_general(
        left_basis, carried_upper, across, preferred_element_type=jnp.float32
    ) + lax.dot_general(left_basis, carried_lower, across, preferred_element_type=jnp.float32)
    left_count = left_basis.shape[0] // lax.axis_size("col")
    left_start = lax.axis_index("col") * left_count
    left_piece = lax.dynamic_slice_in_dim(left_basis, left_start, left_count, 0)
    left_prior = lax.dynamic_slice_in_dim(left_old, left_start, left_count, 0)
    right_count = right_basis.shape[0] // lax.axis_size("row")
    right_start = lax.axis_index("row") * right_count
    right_piece = lax.dynamic_slice_in_dim(right_basis, right_start, right_count, 0)
    right_prior = lax.dynamic_slice_in_dim(right_old, right_start, right_count, 0)
    turn_left_part = lax.dot_general(
        left_piece, left_prior, across, preferred_element_type=jnp.float32
    )
    turn_right_part = lax.dot_general(
        right_piece, right_prior, across, preferred_element_type=jnp.float32
    )
    core, turn_left, turn_right = lax.psum(
        (core_part, turn_left_part, turn_right_part), ("row", "col")
    )
    core_upper, core_lower = split_pair(core)
    lifted_full = jnp.dot(left_basis, core_upper, preferred_element_type=jnp.float32) + jnp.dot(
        left_basis, core_lower, preferred_element_type=jnp.float32
    )
    lifted = lifted_full.astype(jnp.bfloat16)
    rebuilt = lax.dot_general(
        lifted, right_basis, (((1,), (1,)), ((), ())), preferred_element_type=jnp.float32
    )
    error_new = (summed - rebuilt).astype(jnp.bfloat16)
    first_turned = jnp.dot(
        jnp.dot(turn_left, first_old, precision=highest), turn_right.T, precision=highest
    )
    excess = jnp.maximum(second_old - first_old * first_old, 0.0)
    second_turned = (
        jnp.dot(
            jnp.dot(turn_left * turn_left, excess, precision=highest),
            (turn_right * turn_right).T,
            precision=highest,
        )
        + first_turned * first_turned
    )
    first_moment = 0.9 * first_turned + 0.1 * core
    second_moment = 0.999 * second_turned + 0.001 * core * core
    update = first_moment / (jnp.sqrt(second_moment) + 0.01)
    return (error_new, first_moment, second_moment, update)


def solution(mesh):
    return jax.shard_map(
        per_device,
        mesh=mesh,
        in_specs=(
            P(("layer", "row"), "col"),
            P(("layer", "row"), "col"),
            P(("layer", "row"), None),
            P(("layer", "col"), None),
            P("layer", None),
            P("layer", None),
        ),
        out_specs=(
            P(("layer", "row"), "col"),
            P("layer", None),
            P("layer", None),
            P("layer", None),
        ),
        check_vma=False,
    )
```

profile of v0, /device:TPU:0, one launch (start us, length us, event | category | flops | bytes accessed | tf_op | source)
XLA Modules:
  0.0 1060.0 jit_solution(5173255046993698777)
XLA Ops:
  8.8 5.8 fusion.102
  14.7 61.2 %all-reduce.8.cloned.1.call-done = f32[1024,512]{1,0:T(8,128)} async-done(((f32[1024,512]{1,0:T(8,128)}), f32[1024,512]{1,0:T(8,128)}) %all-reduce.8.cloned.1.call-update) | async-done | bytes 2097168 | tf_op jit(solution)/shard_map/psum | solution.py:25
  75.9 5.0 fusion.103
  81.4 87.5 %all-reduce.10.cloned.1.call-done = f32[512,512]{0,1:T(8,128)} async-done(((f32[512,512]{0,1:T(8,128)}), f32[512,512]{0,1:T(8,128)}) %all-reduce.10.cloned.1.call-update) | async-done | bytes 1048592 | tf_op jit(solution)/shard_map/psum | solution.py:26
  174.0 11.7 %cholesky.286 = f32[128,128]{1,0:T(8,128)S(1)} custom-call(f32[128,128]{1,0:T(8,128)S(1)} %cholesky.426), custom_call_target="Cholesky" | custom-call | tf_op jit(solution)/shard_map/jit(cholesky)/cholesky | solution.py:8
  185.8 9.8 custom-call.33
  198.2 11.7 %cholesky.305 = f32[128,128]{1,0:T(8,128)S(1)} custom-call(f32[128,128]{1,0:T(8,128)S(1)} %cholesky.430), custom_call_target="Cholesky" | custom-call | tf_op jit(solution)/shard_map/jit(cholesky)/cholesky | solution.py:8
  209.9 10.0 custom-call.34
  221.5 11.7 %cholesky.326 = f32[128,128]{1,0:T(8,128)S(1)} custom-call(f32[128,128]{1,0:T(8,128)S(1)} %cholesky.435), custom_call_target="Cholesky" | custom-call | tf_op jit(solution)/shard_map/jit(cholesky)/cholesky | solution.py:8
  233.2 9.8 custom-call.35
  244.5 11.7 %cholesky.343 = f32[128,128]{1,0:T(8,128)S(1)} custom-call(f32[128,128]{1,0:T(8,128)S(1)} %convolution_subtract_fusion.9), custom_call_target="Cholesky" | custom-call | tf_op jit(solution)/shard_map/jit(cholesky)/cholesky | solution.py:8
  262.1 11.6 %while.2 = (s32[]{:T(128)}, f32[512,512]{1,0:T(8,128)}, s32[4,2]{0,1:T(2,128)S(1)}, f32[4,128,128]{2,1,0:T(8,128)S(1)}, s32[]{:T(128)}) while((s32[]{:T(128)}, f32[512,512]{1,0:T(8,128)}, s32[4,2]{0,1:T(2,128)S(1)}, f32[4,128,128]{2,1,0:T(8,128)S(1)}, s32[]{:T(128)}) %tuple.61), condition=%wide.while_cond, body=%wide.while_body.sunk | while | flops 2 | bytes 131189 | solution.py:9
  273.7 39.3 %custom-call.28 = f32[4,128,128]{1,2,0:T(8,128)S(1)} custom-call(f32[4,128,128]{2,1,0:T(8,128)S(1)} %get-tuple-element.12), custom_call_target="InvertDiagBlocksLowerTriangular" | custom-call | tf_op jit(solution)/shard_map/jit(_solve_triangular)/triangular_solve | solution.py:9
  321.2 4.0 fusion.23
  325.9 4.4 convolution_bitcast_fusion
  330.4 108.0 %all-reduce.12.cloned.1.call-done = f32[2048,512]{0,1:T(8,128)} async-done(((f32[2048,512]{0,1:T(8,128)}), f32[2048,512]{0,1:T(8,128)}) %all-reduce.12.cloned.1.call-update) | async-done | bytes 4194320 | tf_op jit(solution)/shard_map/psum | solution.py:29
  438.3 7.9 fusion.104
  448.8 42.1 %all-reduce.14.cloned.1.call-done = f32[512,512]{0,1:T(8,128)} async-done(((f32[512,512]{0,1:T(8,128)}), f32[512,512]{0,1:T(8,128)}) %all-reduce.14.cloned.1.call-update) | async-done | bytes 1048592 | tf_op jit(solution)/shard_map/psum | solution.py:30
  496.0 11.7 %cholesky.358 = f32[128,128]{1,0:T(8,128)S(1)} custom-call(f32[128,128]{1,0:T(8,128)S(1)} %cholesky.439), custom_call_target="Cholesky" | custom-call | tf_op jit(solution)/shard_map/jit(cholesky)/cholesky | solution.py:8
  507.9 9.8 custom-call.36
  520.9 11.7 %cholesky.377 = f32[128,128]{1,0:T(8,128)S(1)} custom-call(f32[128,128]{1,0:T(8,128)S(1)} %cholesky.443), custom_call_target="Cholesky" | custom-call | tf_op jit(solution)/shard_map/jit(cholesky)/cholesky | solution.py:8
  532.6 10.2 custom-call.37
  545.9 13.2 %cholesky.398 = f32[128,128]{1,0:T(8,128)} custom-call(f32[128,128]{1,0:T(8,128)} %cholesky.448), custom_call_target="Cholesky" | custom-call | tf_op jit(solution)/shard_map/jit(cholesky)/cholesky | solution.py:8
  560.6 11.3 %custom-call.38 = f32[1,128,128]{1,2,0:T(8,128)} custom-call(f32[1,128,128]{2,1,0:T(8,128)} %get-tuple-element.49), custom_call_target="InvertDiagBlocksLowerTriangular" | custom-call | tf_op jit(solution)/shard_map/jit(cholesky)/cholesky | solution.py:8
  574.1 11.9 %cholesky.415 = f32[128,128]{1,0:T(8,128)S(1)} custom-call(f32[128,128]{1,0:T(8,128)S(1)} %convolution_subtract_fusion.8), custom_call_target="Cholesky" | custom-call | tf_op jit(solution)/shard_map/jit(cholesky)/cholesky | solution.py:8
  592.2 11.6 %while.3 = (s32[]{:T(128)}, f32[512,512]{1,0:T(8,128)}, s32[4,2]{0,1:T(2,128)S(1)}, f32[4,128,128]{2,1,0:T(8,128)S(1)}, s32[]{:T(128)}) while((s32[]{:T(128)}, f32[512,512]{1,0:T(8,128)}, s32[4,2]{0,1:T(2,128)S(1)}, f32[4,128,128]{2,1,0:T(8,128)S(1)}, s32[]{:T(128)}) %tuple.78), condition=%wide.while_cond.1, body=%wide.while_body.1.sunk | while | flops 2 | bytes 131189 | solution.py:9
  603.8 39.3 %custom-call.29 = f32[4,128,128]{1,2,0:T(8,128)S(1)} custom-call(f32[4,128,128]{2,1,0:T(8,128)S(1)} %get-tuple-element.20), custom_call_target="InvertDiagBlocksLowerTriangular" | custom-call | tf_op jit(solution)/shard_map/jit(_solve_triangular)/triangular_solve | solution.py:9
  665.1 362.9 %all-reduce.16.cloned.1.call-done = (f32[512,512]{1,0:T(8,128)}, f32[512,512]{1,0:T(8,128)}, f32[512,512]{1,0:T(8,128)}) async-done(((f32[512,512]{1,0:T(8,128)}, f32[512,512]{1,0:T(8,128)}, f32[512,512]{1,0:T(8,128)}), (f32[512,512]{1,0:T(8,128)}, f32[512,512]{1,0:T(8,128)}, f32[512,512]{1,0:T(8,128)})) %all-reduce.16.cloned.1.call-update) | async-done | bytes 3145744 | tf_op jit(solution)/shard_map/psum | solution.py:53
  1028.0 3.5 fusion.55
  1031.6 10.4 subtract_convert_fusion
  1042.0 3.2 fusion.105
  1049.1 4.1 add_divide_fusion
  (153 shorter events, 95.3 us)
Async XLA Ops:
  7.2 1.6 copy-start
  7.2 68.7 %all-reduce.8.cloned.1.call-start = ((), (), s32[]{:S(2)}) async-start(), calls=%async_computation | async-start | bytes 4194304 | tf_op jit(solution)/shard_map/psum | solution.py:25
  14.6 154.3 %all-reduce.10.cloned.1.call-start = ((), (), s32[]{:S(2)}) async-start(), calls=%async_computation.1 | async-start | bytes 2097152 | tf_op jit(solution)/shard_map/psum | solution.py:26
  80.9 357.4 %all-reduce.12.cloned.1.call-start = ((), (), s32[]{:S(2)}) async-start(), calls=%async_computation.2 | async-start | bytes 8388608 | tf_op jit(solution)/shard_map/psum | solution.py:29
  168.9 2.6 copy-start.5
  173.0 1.0 copy-start.8
  313.0 4.7 copy-start.2
  314.9 131.6 %copy-start.16 = (bf16[128,1024]{1,0:T(8,128)(2,1)}, bf16[128,1024]{1,0:T(8,128)(2,1)S(1)}, u32[]{:S(2)}) copy-start(bf16[128,1024]{1,0:T(8,128)(2,1)S(1)} %get-tuple-element.72) | copy-start | bytes 786436
  317.7 128.8 %copy-start.18 = (bf16[128,1024]{1,0:T(8,128)(2,1)}, bf16[128,1024]{1,0:T(8,128)(2,1)S(1)}, u32[]{:S(2)}) copy-start(bf16[128,1024]{1,0:T(8,128)(2,1)S(1)} %get-tuple-element.70) | copy-start | bytes 786436
  320.5 5.3 copy-start.24
  321.2 125.3 %copy-start.20 = (bf16[128,1024]{1,0:T(8,128)(2,1)}, bf16[128,1024]{1,0:T(8,128)(2,1)S(1)}, u32[]{:S(2)}) copy-start(bf16[128,1024]{1,0:T(8,128)(2,1)S(1)} %get-tuple-element.68) | copy-start | bytes 786436
  330.3 160.6 %all-reduce.14.cloned.1.call-start = ((), (), s32[]{:S(2)}) async-start(), calls=%async_computation.3 | async-start | bytes 2097152 | tf_op jit(solution)/shard_map/psum | solution.py:30
  446.2 581.8 %all-reduce.16.cloned.1.call-start = ((), (), s32[]{:S(2)}) async-start(), calls=%async_computation.4 | async-start | bytes 6291456 | tf_op jit(solution)/shard_map/psum | solution.py:53
  490.9 2.6 copy-start.4
  495.0 1.0 copy-start.9
  520.2 0.7 copy-start.22
  645.4 11.5 %copy-start.11 = (bf16[128,2048]{1,0:T(8,128)(2,1)}, bf16[128,2048]{1,0:T(8,128)(2,1)S(1)}, u32[]{:S(2)}) copy-start(bf16[128,2048]{1,0:T(8,128)(2,1)S(1)} %get-tuple-element.80) | copy-start | bytes 1572868
  645.4 3.6 copy-start.1
  648.9 7.9 copy-start.12
  652.3 4.6 copy-start.13
  652.3 5.1 copy-start.25
  656.6 0.8 copy-start.10
  656.6 2.4 copy-start.23
  659.0 2.4 copy-start.17
  659.0 2.4 copy-start.19
  659.0 2.4 copy-start.21
  1031.6 10.5 copy-start.6
  1042.0 3.2 copy-start.7
  1042.0 3.2 copy-start.15
  1045.2 2.0 copy-start.3
  1047.2 1.9 copy-start.14
Sparse Core Ops, SparseCore 0:
  14.7 61.0 all-reduce.7
  81.0 87.8 all-reduce.9
  330.4 107.8 all-reduce.11
  446.4 44.5 all-reduce.13
  665.3 362.7 all-reduce.15
where the time goes:
time: 1060 us
  waiting for transfers between devices  662 us (62%)
  other arithmetic  247 us (23%)
  matrix products  95.3 us (9%)
  local copies, waits for them, and re-layouts  35.5 us (3%)
  between operations  19.7 us (2%)
    psum x1, waiting for transfers between devices, per_device(): lax.psum((core_part, turn_left_part, turn_right_part), ('row', 'col'))  363 us
    another operation x29, other arithmetic, solve_rows(): factor = jnp.linalg.cholesky(gram)  162 us
    psum x1, waiting for transfers between devices, per_device(): right_image = lax.psum(right_part, 'row')  108 us
    psum x1, waiting for transfers between devices, per_device(): left_gram = lax.psum(gram_of(left_image), 'row')  87.5 us
    another operation x7, other arithmetic, solve_rows(): jax.scipy.linalg.solve_triangular(factor, image.T, lower=True)  81.5 us
    psum x1, waiting for transfers between devices, per_device(): lax.psum(jnp.dot(grad, right_old, preferred_element_type=jnp.float32), 'c...  61.2 us
    psum x1, waiting for transfers between devices, per_device(): right_gram = lax.psum(gram_of(right_image), 'col')  42.1 us
    another operation x14, matrix products, solve_rows(): jax.scipy.linalg.solve_triangular(factor, image.T, lower=True)  26.1 us
  transfers between devices with their start and end apart: 5, of which 5 were waited for; matrix products, arithmetic and copies ran while one was open for 0% of the time, Pallas kernels for 0%

commit v1 on v0

--- a/solution.py
+++ b/solution.py
@@ -23,7 +23,7 @@
     highest = lax.Precision.HIGHEST
     across = (((0,), (0,)), ((), ()))
     left_image = lax.psum(jnp.dot(grad, right_old, preferred_element_type=jnp.float32), "col")
-    left_gram = lax.psum(gram_of(left_image), "row")
+    left_gram = jnp.sum(lax.all_gather(gram_of(left_image), "row"), axis=0)
     left_basis = solve_rows(left_image, left_gram)
     right_part = lax.dot_general(grad, left_basis, across, preferred_element_type=jnp.float32)
     right_image = lax.psum(right_part, "row")

time: 1060 us -> 1090 us (1.028)
  waiting for transfers between devices: 662 us -> 682 us
    all_gather x0 -> x1, waiting for transfers between devices: none -> 108 us  [per_device(): left_gram = jnp.sum(lax.all_gather(gram_of(left_image), 'row'), axis=0)]
    psum x1 -> x0, waiting for transfers between devices: 87.5 us -> none  [per_device(): left_gram = lax.psum(gram_of(left_image), 'row')]
where the time goes in v1:
time: 1090 us; the launch traced here: 1080 us
  waiting for transfers between devices  682 us (63%)
  other arithmetic  251 us (23%)
  matrix products  95.3 us (9%)
  local copies, waits for them, and re-layouts  34.2 us (3%)
  between operations  19.9 us (2%)
    psum x1, waiting for transfers between devices, per_device(): lax.psum((core_part, turn_left_part, turn_right_part), ('row', 'col'))  363 us
    another operation x29, other arithmetic, solve_rows(): factor = jnp.linalg.cholesky(gram)  163 us
    all_gather x1, waiting for transfers between devices, per_device(): left_gram = jnp.sum(lax.all_gather(gram_of(left_image), 'row'), axis=0)  108 us
    psum x1, waiting for transfers between devices, per_device(): right_image = lax.psum(right_part, 'row')  108 us
    another operation x7, other arithmetic, solve_rows(): jax.scipy.linalg.solve_triangular(factor, image.T, lower=True)  81.1 us
    psum x1, waiting for transfers between devices, per_device(): lax.psum(jnp.dot(grad, right_old, preferred_element_type=jnp.float32), 'c...  61.2 us
    psum x1, waiting for transfers between devices, per_device(): right_gram = lax.psum(gram_of(right_image), 'col')  42.3 us
    another operation x14, matrix products, solve_rows(): jax.scipy.linalg.solve_triangular(factor, image.T, lower=True)  26.1 us
  transfers between devices with their start and end apart: 5, of which 5 were waited for; matrix products, arithmetic and copies ran while one was open for 0% of the time, Pallas kernels for 0%

profile of v1, /device:TPU:0, one launch (start us, length us, event | category | flops | bytes accessed | tf_op | source)
XLA Modules:
  0.0 1083.9 jit_solution(17705203934913090651)
XLA Ops:
  8.8 5.8 fusion.102
  14.7 61.2 %all-reduce.7.cloned.1.call-done = f32[1024,512]{1,0:T(8,128)} async-done(((f32[1024,512]{1,0:T(8,128)}), f32[1024,512]{1,0:T(8,128)}) %all-reduce.7.cloned.1.call-update) | async-done | bytes 2097168 | tf_op jit(solution)/shard_map/psum | solution.py:25
  75.9 5.0 fusion.103
  81.4 107.9 %all-gather.3.cloned.1.call-done = f32[4096,512]{1,0:T(8,128)} async-done(((f32[512,512]{1,0:T(8,128)}), f32[4096,512]{1,0:T(8,128)}) %all-gather.3.cloned.1.call-update) | async-done | bytes 8388624 | tf_op jit(solution)/shard_map/all_gather | solution.py:26
  189.4 4.5 reduce_sum.9
  197.6 11.7 %cholesky.286 = f32[128,128]{1,0:T(8,128)S(1)} custom-call(f32[128,128]{1,0:T(8,128)S(1)} %cholesky.426), custom_call_target="Cholesky" | custom-call | tf_op jit(solution)/shard_map/jit(cholesky)/cholesky | solution.py:8
  209.5 9.8 custom-call.33
  221.8 11.8 %cholesky.305 = f32[128,128]{1,0:T(8,128)S(1)} custom-call(f32[128,128]{1,0:T(8,128)S(1)} %cholesky.430), custom_call_target="Cholesky" | custom-call | tf_op jit(solution)/shard_map/jit(cholesky)/cholesky | solution.py:8
  233.7 9.8 custom-call.34
  245.0 11.7 %cholesky.326 = f32[128,128]{1,0:T(8,128)S(1)} custom-call(f32[128,128]{1,0:T(8,128)S(1)} %cholesky.435), custom_call_target="Cholesky" | custom-call | tf_op jit(solution)/shard_map/jit(cholesky)/cholesky | solution.py:8
  256.8 9.8 custom-call.35
  268.1 12.1 %cholesky.343 = f32[128,128]{1,0:T(8,128)S(1)} custom-call(f32[128,128]{1,0:T(8,128)S(1)} %convolution_subtract_fusion.9), custom_call_target="Cholesky" | custom-call | tf_op jit(solution)/shard_map/jit(cholesky)/cholesky | solution.py:8
  285.8 11.6 %while.2 = (s32[]{:T(128)}, f32[512,512]{1,0:T(8,128)}, s32[4,2]{0,1:T(2,128)S(1)}, f32[4,128,128]{2,1,0:T(8,128)S(1)}, s32[]{:T(128)}) while((s32[]{:T(128)}, f32[512,512]{1,0:T(8,128)}, s32[4,2]{0,1:T(2,128)S(1)}, f32[4,128,128]{2,1,0:T(8,128)S(1)}, s32[]{:T(128)}) %tuple.61), condition=%wide.while_cond, body=%wide.while_body.sunk | while | flops 2 | bytes 131189 | solution.py:9
  297.4 39.3 %custom-call.28 = f32[4,128,128]{1,2,0:T(8,128)S(1)} custom-call(f32[4,128,128]{2,1,0:T(8,128)S(1)} %get-tuple-element.12), custom_call_target="InvertDiagBlocksLowerTriangular" | custom-call | tf_op jit(solution)/shard_map/jit(_solve_triangular)/triangular_solve | solution.py:9
  344.9 4.0 fusion.23
  349.6 4.4 convolution_bitcast_fusion
  354.2 107.6 %all-reduce.9.cloned.1.call-done = f32[2048,512]{0,1:T(8,128)} async-done(((f32[2048,512]{0,1:T(8,128)}), f32[2048,512]{0,1:T(8,128)}) %all-reduce.9.cloned.1.call-update) | async-done | bytes 4194320 | tf_op jit(solution)/shard_map/psum | solution.py:29
  461.8 7.9 fusion.104
  472.1 42.3 %all-reduce.11.cloned.1.call-done = f32[512,512]{0,1:T(8,128)} async-done(((f32[512,512]{0,1:T(8,128)}), f32[512,512]{0,1:T(8,128)}) %all-reduce.11.cloned.1.call-update) | async-done | bytes 1048592 | tf_op jit(solution)/shard_map/psum | solution.py:30
  519.5 11.7 %cholesky.358 = f32[128,128]{1,0:T(8,128)S(1)} custom-call(f32[128,128]{1,0:T(8,128)S(1)} %cholesky.439), custom_call_target="Cholesky" | custom-call | tf_op jit(solution)/shard_map/jit(cholesky)/cholesky | solution.py:8
  531.4 9.8 custom-call.36
  544.4 11.7 %cholesky.377 = f32[128,128]{1,0:T(8,128)S(1)} custom-call(f32[128,128]{1,0:T(8,128)S(1)} %cholesky.443), custom_call_target="Cholesky" | custom-call | tf_op jit(solution)/shard_map/jit(cholesky)/cholesky | solution.py:8
  556.2 10.2 custom-call.37
  569.5 13.2 %cholesky.398 = f32[128,128]{1,0:T(8,128)} custom-call(f32[128,128]{1,0:T(8,128)} %cholesky.448), custom_call_target="Cholesky" | custom-call | tf_op jit(solution)/shard_map/jit(cholesky)/cholesky | solution.py:8
  584.1 11.3 %custom-call.38 = f32[1,128,128]{1,2,0:T(8,128)} custom-call(f32[1,128,128]{2,1,0:T(8,128)} %get-tuple-element.49), custom_call_target="InvertDiagBlocksLowerTriangular" | custom-call | tf_op jit(solution)/shard_map/jit(cholesky)/cholesky | solution.py:8
  597.7 11.9 %cholesky.415 = f32[128,128]{1,0:T(8,128)S(1)} custom-call(f32[128,128]{1,0:T(8,128)S(1)} %convolution_subtract_fusion.8), custom_call_target="Cholesky" | custom-call | tf_op jit(solution)/shard_map/jit(cholesky)/cholesky | solution.py:8
  615.9 11.6 %while.3 = (s32[]{:T(128)}, f32[512,512]{1,0:T(8,128)}, s32[4,2]{0,1:T(2,128)S(1)}, f32[4,128,128]{2,1,0:T(8,128)S(1)}, s32[]{:T(128)}) while((s32[]{:T(128)}, f32[512,512]{1,0:T(8,128)}, s32[4,2]{0,1:T(2,128)S(1)}, f32[4,128,128]{2,1,0:T(8,128)S(1)}, s32[]{:T(128)}) %tuple.78), condition=%wide.while_cond.1, body=%wide.while_body.1.sunk | while | flops 2 | bytes 131189 | solution.py:9
  627.5 39.3 %custom-call.29 = f32[4,128,128]{1,2,0:T(8,128)S(1)} custom-call(f32[4,128,128]{2,1,0:T(8,128)S(1)} %get-tuple-element.20), custom_call_target="InvertDiagBlocksLowerTriangular" | custom-call | tf_op jit(solution)/shard_map/jit(_solve_triangular)/triangular_solve | solution.py:9
  688.9 363.1 %all-reduce.13.cloned.1.call-done = (f32[512,512]{1,0:T(8,128)}, f32[512,512]{1,0:T(8,128)}, f32[512,512]{1,0:T(8,128)}) async-done(((f32[512,512]{1,0:T(8,128)}, f32[512,512]{1,0:T(8,128)}, f32[512,512]{1,0:T(8,128)}), (f32[512,512]{1,0:T(8,128)}, f32[512,512]{1,0:T(8,128)}, f32[512,512]{1,0:T(8,128)})) %all-reduce.13.cloned.1.call-update) | async-done | bytes 3145744 | tf_op jit(solution)/shard_map/psum | solution.py:53
  1052.0 3.5 fusion.55
  1055.5 10.4 subtract_convert_fusion
  1073.1 4.1 add_divide_fusion
  (152 shorter events, 96.9 us)
Async XLA Ops:
  7.2 1.6 copy-start
  7.2 68.7 %all-reduce.7.cloned.1.call-start = ((), (), s32[]{:S(2)}) async-start(), calls=%async_computation | async-start | bytes 4194304 | tf_op jit(solution)/shard_map/psum | solution.py:25
  14.6 174.8 %all-gather.3.cloned.1.call-start = ((), (), s32[]{:S(2)}) async-start(), calls=%async_computation.3 | async-start | bytes 9437184 | tf_op jit(solution)/shard_map/all_gather | solution.py:26
  80.9 380.9 %all-reduce.9.cloned.1.call-start = ((), (), s32[]{:S(2)}) async-start(), calls=%async_computation.1 | async-start | bytes 8388608 | tf_op jit(solution)/shard_map/psum | solution.py:29
  196.6 1.0 copy-start.7
  336.7 4.7 copy-start.2
  338.6 131.2 %copy-start.15 = (bf16[128,1024]{1,0:T(8,128)(2,1)}, bf16[128,1024]{1,0:T(8,128)(2,1)S(1)}, u32[]{:S(2)}) copy-start(bf16[128,1024]{1,0:T(8,128)(2,1)S(1)} %get-tuple-element.72) | copy-start | bytes 786436
  341.4 128.4 %copy-start.17 = (bf16[128,1024]{1,0:T(8,128)(2,1)}, bf16[128,1024]{1,0:T(8,128)(2,1)S(1)}, u32[]{:S(2)}) copy-start(bf16[128,1024]{1,0:T(8,128)(2,1)S(1)} %get-tuple-element.70) | copy-start | bytes 786436
  344.2 5.3 copy-start.23
  344.9 124.9 %copy-start.19 = (bf16[128,1024]{1,0:T(8,128)(2,1)}, bf16[128,1024]{1,0:T(8,128)(2,1)S(1)}, u32[]{:S(2)}) copy-start(bf16[128,1024]{1,0:T(8,128)(2,1)S(1)} %get-tuple-element.68) | copy-start | bytes 786436
  354.0 160.4 %all-reduce.11.cloned.1.call-start = ((), (), s32[]{:S(2)}) async-start(), calls=%async_computation.2 | async-start | bytes 2097152 | tf_op jit(solution)/shard_map/psum | solution.py:30
  469.7 582.3 %all-reduce.13.cloned.1.call-start = ((), (), s32[]{:S(2)}) async-start(), calls=%async_computation.4 | async-start | bytes 6291456 | tf_op jit(solution)/shard_map/psum | solution.py:53
  514.5 2.6 copy-start.4
  518.5 1.0 copy-start.8
  543.7 0.7 copy-start.21
  669.1 11.5 %copy-start.10 = (bf16[128,2048]{1,0:T(8,128)(2,1)}, bf16[128,2048]{1,0:T(8,128)(2,1)S(1)}, u32[]{:S(2)}) copy-start(bf16[128,2048]{1,0:T(8,128)(2,1)S(1)} %get-tuple-element.80) | copy-start | bytes 1572868
  669.1 3.6 copy-start.1
  672.7 7.9 copy-start.11
  676.1 4.6 copy-start.12
  676.1 5.1 copy-start.24
  680.3 0.8 copy-start.9
  680.3 2.4 copy-start.22
  682.7 2.4 copy-start.16
  682.7 2.4 copy-start.18
  682.7 2.4 copy-start.20
  1055.5 10.4 copy-start.5
  1065.9 3.2 copy-start.6
  1065.9 3.2 copy-start.14
  1069.2 2.0 copy-start.3
  1071.2 1.9 copy-start.13
Sparse Core Ops, SparseCore 0:
  14.7 61.0 all-reduce.6
  81.0 108.2 all-gather.2
  354.1 107.6 all-reduce.8
  469.9 44.5 all-reduce.10
  689.0 362.9 all-reduce.12
